TPU v7x, 32 devices: a whole 2x2x4 slice. The times are simulated.
32 devices in a mesh: adapter: 8 (over z, x), feature: 4 (over y, core).
Axes of the slice: x: 2, y: 2, z: 4, core: 2. Of those that a mesh axis runs over, the one named last changes fastest.
Arguments:
- adapter_down: bfloat16 [128, 16, 8192], P('adapter', None, 'feature'), may hold values from -6 to 6
- adapter_up: bfloat16 [128, 16, 8192], P('adapter', None, 'feature'), may hold values from -6 to 6
- fisher: float32 [128], P('adapter'), may hold values from 0.1 to 10
- init_v: float32 [8192, 64], P('feature'), may hold values from -0.0625 to 0.0625
- init_u: float32 [8192, 64], P('feature'), may hold values from -0.0625 to 0.0625
- prompt_rows: bfloat16 [4096, 8192], P('adapter', 'feature'), may hold values from -6 to 6
- request_ids: int32 [32], P('adapter'), may hold values from 0 to 127
Outputs:
- served: bfloat16 [4096, 8192], P('adapter', 'feature')
All inputs are finite; a program needn't handle non-finite values.
Results may differ from a plain program's by a relative error of at most 0.025.
Values may be sent and summed in bfloat16 or wider, within the bound.
A program may use at most 64 MiB of HBM per device.

v0:
```python
import jax
import jax.numpy as jnp
from jax import lax
from jax.sharding import PartitionSpec as P

SWEEPS = 3
highest = lax.Precision.HIGHEST


def project(adapter_stack, basis_low):
    flat = adapter_stack.reshape(-1, adapter_stack.shape[-1])
    result = jnp.dot(flat, basis_low, preferred_element_type=jnp.float32)
    return result.reshape(adapter_stack.shape[0], adapter_stack.shape[1], -1)


def core_of(cols_q, rows_p):
    return jnp.einsum("irk,irl->ikl", cols_q, rows_p, precision=highest)


def numerator(adapter_stack, weighted):
    flat = adapter_stack.reshape(-1, adapter_stack.shape[-1])
    terms = weighted.reshape(-1, weighted.shape[-1])
    return lax.dot_general(
        flat, terms, (((0,), (0,)), ((), ())), preferred_element_type=jnp.float32
    )


def solve_with(gram_sum, matrix):
    factor = jnp.linalg.cholesky(gram_sum)
    return lax.linalg.triangular_solve(
        factor, matrix, left_side=False, lower=True, transpose_a=True
    )


def renew(local_term):
    full_term = lax.psum(local_term, "adapter")
    gram_sum = lax.psum(jnp.dot(full_term.T, full_term, precision=highest), "feature")
    return solve_with(gram_sum, full_term)


def down_sum(adapter_down, basis_v):
    return lax.psum(project(adapter_down, basis_v.astype(jnp.bfloat16)), "feature")


def up_sum(adapter_up, basis_u):
    return lax.psum(project(adapter_up, basis_u.astype(jnp.bfloat16)), "feature")


def on_device(adapter_down, adapter_up, fisher, init_v, init_u, prompt_rows, request_ids):
    basis_v = init_v
    basis_u = init_u
    weights = fisher[:, None, None]
    cols_q = up_sum(adapter_up, basis_u)
    for sweep_index in range(SWEEPS):
        rows_p = down_sum(adapter_down, basis_v)
        core_stack = core_of(cols_q, rows_p)
        weighted = (
            weights * jnp.einsum("irl,ikl->irk", rows_p, core_stack, precision=highest)
        ).astype(jnp.bfloat16)
        basis_u = renew(numerator(adapter_up, weighted))
        cols_q = up_sum(adapter_up, basis_u)
        core_stack = core_of(cols_q, rows_p)
        weighted = (
            weights * jnp.einsum("irk,ikl->irl", cols_q, core_stack, precision=highest)
        ).astype(jnp.bfloat16)
        basis_v = renew(numerator(adapter_down, weighted))
    rows_p = down_sum(adapter_down, basis_v)
    final_cores = core_of(cols_q, rows_p).astype(jnp.bfloat16)
    count_local = final_cores.shape[0]
    basis_width = final_cores.shape[1]
    flat_cores = final_cores.reshape(count_local, basis_width * basis_width)
    every_core = lax.all_gather(flat_cores, "adapter", axis=0, tiled=True)
    onehot = (
        request_ids[:, None] == jnp.arange(every_core.shape[0], dtype=jnp.int32)[None, :]
    ).astype(jnp.bfloat16)
    own_cores = jnp.dot(onehot, every_core, preferred_element_type=jnp.float32).astype(jnp.bfloat16)
    partial_rows = jnp.dot(
        prompt_rows, basis_v.astype(jnp.bfloat16), preferred_element_type=jnp.float32
    )
    hidden = lax.psum(partial_rows, "feature").astype(jnp.bfloat16)
    blocks = own_cores.shape[0]
    blocked = hidden.reshape(blocks, -1, basis_width)
    mixed_rows = jnp.einsum(
        "bnl,bkl->bnk",
        blocked,
        own_cores.reshape(blocks, basis_width, basis_width),
        preferred_element_type=jnp.float32,
    ).astype(jnp.bfloat16)
    served = jnp.dot(
        mixed_rows.reshape(-1, basis_width),
        basis_u.astype(jnp.bfloat16).T,
        preferred_element_type=jnp.float32,
    )
    return served.astype(jnp.bfloat16)


def solution(mesh):
    placed = (
        P("adapter", None, "feature"),
        P("adapter", None, "feature"),
        P("adapter"),
        P("feature", None),
        P("feature", None),
        P("adapter", "feature"),
        P("adapter"),
    )
    return jax.shard_map(
        on_device, mesh=mesh, in_specs=placed, out_specs=P("adapter", "feature"), check_vma=False
    )
```

profile of v0, /device:TPU:0, one launch (start us, length us, event | category | flops | bytes accessed | tf_op | source)
XLA Modules:
  0.0 935.1 jit_solution(6961525895619962585)
XLA Ops:
  6.5 2.6 fusion.15
  9.1 2.1 fusion.13
  11.3 35.2 %all-reduce.40.cloned.1.call-done = (f32[16,16,64]{2,1,0:T(8,128)}, f32[16,16,64]{2,1,0:T(8,128)}) async-done(((f32[16,16,64]{2,1,0:T(8,128)}, f32[16,16,64]{2,1,0:T(8,128)}), (f32[16,16,64]{2,1,0:T(8,128)}, f32[16,16,64]{2,1,0:T(8,128)})) %all-reduce.40.cloned.1.call-update) | async-done | bytes 131088 | tf_op jit(solution)/shard_map/psum | solution.py:42
  46.5 2.0 fusion.52
  48.5 1.8 fusion.6
  51.5 72.8 %all-reduce.16.cloned.1.call-done = f32[2048,64]{0,1:T(8,128)} async-done(((f32[2048,64]{0,1:T(8,128)}), f32[2048,64]{0,1:T(8,128)}) %all-reduce.16.cloned.1.call-update) | async-done | bytes 524304 | tf_op jit(solution)/shard_map/psum | solution.py:36
  124.3 1.8 fusion.53
  126.1 10.3 %psum.150 = f32[64,64]{0,1:T(8,128)S(1)} all-reduce(f32[64,64]{0,1:T(8,128)S(1)} %fusion.53), channel_id=1, replica_groups=mesh['adapter'=8,'feature'=4] {'feature'}, use_global_device_ids=true, to_apply=%region_3.0 | all-reduce | flops 4096 | bytes 32768 | tf_op jit(solution)/shard_map/psum | solution.py:37
  136.4 5.8 cholesky.104
  143.6 4.9 custom-call.10
  148.5 1.7 fusion
  151.5 31.2 %all-reduce.18.cloned.1.call-done = f32[16,16,64]{2,1,0:T(8,128)} async-done(((f32[16,16,64]{2,1,0:T(8,128)}), f32[16,16,64]{2,1,0:T(8,128)}) %all-reduce.18.cloned.1.call-update) | async-done | bytes 65552 | tf_op jit(solution)/shard_map/psum | solution.py:46
  182.7 1.9 fusion.54
  186.1 2.3 convolution_bitcast_fusion.10
  188.5 72.9 %all-reduce.20.cloned.1.call-done = f32[2048,64]{0,1:T(8,128)} async-done(((f32[2048,64]{0,1:T(8,128)}), f32[2048,64]{0,1:T(8,128)}) %all-reduce.20.cloned.1.call-update) | async-done | bytes 524304 | tf_op jit(solution)/shard_map/psum | solution.py:36
  261.4 1.8 fusion.55
  263.2 10.3 %psum.153 = f32[64,64]{0,1:T(8,128)S(1)} all-reduce(f32[64,64]{0,1:T(8,128)S(1)} %fusion.55), channel_id=1, replica_groups=mesh['adapter'=8,'feature'=4] {'feature'}, use_global_device_ids=true, to_apply=%region_8.11 | all-reduce | flops 4096 | bytes 32768 | tf_op jit(solution)/shard_map/psum | solution.py:37
  273.5 5.8 cholesky.115
  280.7 4.9 custom-call.11
  285.6 1.7 fusion.1
  287.3 1.7 convolution_bitcast_fusion.17
  290.0 31.1 %all-reduce.22.cloned.1.call-done = f32[16,16,64]{2,1,0:T(8,128)} async-done(((f32[16,16,64]{2,1,0:T(8,128)}), f32[16,16,64]{2,1,0:T(8,128)}) %all-reduce.22.cloned.1.call-update) | async-done | bytes 65552 | tf_op jit(solution)/shard_map/psum | solution.py:42
  321.0 1.9 fusion.56
  323.0 1.8 fusion.8
  326.0 72.9 %all-reduce.24.cloned.1.call-done = f32[2048,64]{0,1:T(8,128)} async-done(((f32[2048,64]{0,1:T(8,128)}), f32[2048,64]{0,1:T(8,128)}) %all-reduce.24.cloned.1.call-update) | async-done | bytes 524304 | tf_op jit(solution)/shard_map/psum | solution.py:36
  398.9 1.8 fusion.57
  400.7 10.3 %psum.156 = f32[64,64]{0,1:T(8,128)S(1)} all-reduce(f32[64,64]{0,1:T(8,128)S(1)} %fusion.57), channel_id=1, replica_groups=mesh['adapter'=8,'feature'=4] {'feature'}, use_global_device_ids=true, to_apply=%region_11.14 | all-reduce | flops 4096 | bytes 32768 | tf_op jit(solution)/shard_map/psum | solution.py:37
  411.0 5.8 cholesky.126
  418.2 4.9 custom-call.12
  423.1 1.7 fusion.2
  426.1 31.2 %all-reduce.26.cloned.1.call-done = f32[16,16,64]{2,1,0:T(8,128)} async-done(((f32[16,16,64]{2,1,0:T(8,128)}), f32[16,16,64]{2,1,0:T(8,128)}) %all-reduce.26.cloned.1.call-update) | async-done | bytes 65552 | tf_op jit(solution)/shard_map/psum | solution.py:46
  457.3 1.9 fusion.58
  460.7 2.3 convolution_bitcast_fusion.8
  463.1 72.9 %all-reduce.28.cloned.1.call-done = f32[2048,64]{0,1:T(8,128)} async-done(((f32[2048,64]{0,1:T(8,128)}), f32[2048,64]{0,1:T(8,128)}) %all-reduce.28.cloned.1.call-update) | async-done | bytes 524304 | tf_op jit(solution)/shard_map/psum | solution.py:36
  536.0 1.8 fusion.59
  537.8 10.3 %psum.159 = f32[64,64]{0,1:T(8,128)S(1)} all-reduce(f32[64,64]{0,1:T(8,128)S(1)} %fusion.59), channel_id=1, replica_groups=mesh['adapter'=8,'feature'=4] {'feature'}, use_global_device_ids=true, to_apply=%region_14.17 | all-reduce | flops 4096 | bytes 32768 | tf_op jit(solution)/shard_map/psum | solution.py:37
  548.1 5.8 cholesky.137
  555.3 4.9 custom-call.13
  560.2 1.7 fusion.3
  564.4 31.2 %all-reduce.30.cloned.1.call-done = f32[16,16,64]{2,1,0:T(8,128)} async-done(((f32[16,16,64]{2,1,0:T(8,128)}), f32[16,16,64]{2,1,0:T(8,128)}) %all-reduce.30.cloned.1.call-update) | async-done | bytes 65552 | tf_op jit(solution)/shard_map/psum | solution.py:42
  595.6 1.9 fusion.60
  597.5 1.8 fusion.10
  600.8 72.7 %all-reduce.32.cloned.1.call-done = f32[2048,64]{0,1:T(8,128)} async-done(((f32[2048,64]{0,1:T(8,128)}), f32[2048,64]{0,1:T(8,128)}) %all-reduce.32.cloned.1.call-update) | async-done | bytes 524304 | tf_op jit(solution)/shard_map/psum | solution.py:36
  673.5 1.8 fusion.61
  675.2 10.3 %psum.162 = f32[64,64]{0,1:T(8,128)S(1)} all-reduce(f32[64,64]{0,1:T(8,128)S(1)} %fusion.61), channel_id=1, replica_groups=mesh['adapter'=8,'feature'=4] {'feature'}, use_global_device_ids=true, to_apply=%region_17.20 | all-reduce | flops 4096 | bytes 32768 | tf_op jit(solution)/shard_map/psum | solution.py:37
  685.6 5.8 cholesky.148
  692.8 5.5 custom-call.14
  698.3 1.7 fusion.4
  701.1 1.7 copy.37
  702.8 31.2 %all-reduce.34.cloned.1.call-done = f32[16,16,64]{2,1,0:T(8,128)} async-done(((f32[16,16,64]{2,1,0:T(8,128)}), f32[16,16,64]{2,1,0:T(8,128)}) %all-reduce.34.cloned.1.call-update) | async-done | bytes 65552 | tf_op jit(solution)/shard_map/psum | solution.py:46
  734.1 1.9 fusion.62
  738.7 72.7 %all-reduce.36.cloned.1.call-done = f32[2048,64]{0,1:T(8,128)} async-done(((f32[2048,64]{0,1:T(8,128)}), f32[2048,64]{0,1:T(8,128)}) %all-reduce.36.cloned.1.call-update) | async-done | bytes 524304 | tf_op jit(solution)/shard_map/psum | solution.py:36
  811.4 2.4 fusion.63
  813.8 11.4 %psum.165 = f32[64,64]{0,1:T(8,128)} all-reduce(f32[64,64]{0,1:T(8,128)} %fusion.63), channel_id=1, replica_groups=mesh['adapter'=8,'feature'=4] {'feature'}, use_global_device_ids=true, to_apply=%region_20.23 | all-reduce | flops 4096 | bytes 32768 | tf_op jit(solution)/shard_map/psum | solution.py:37
  828.0 7.2 cholesky.159
  836.7 2.0 fusion.28
  838.7 6.3 custom-call.15
  845.0 1.7 fusion.5
  850.1 31.3 %all-reduce.38.cloned.1.call-done = f32[16,16,64]{2,1,0:T(8,128)} async-done(((f32[16,16,64]{2,1,0:T(8,128)}), f32[16,16,64]{2,1,0:T(8,128)}) %all-reduce.38.cloned.1.call-update) | async-done | bytes 65552 | tf_op jit(solution)/shard_map/psum | solution.py:42
  881.4 1.9 convolution_convert_fusion.2
  884.3 1.7 convolution_bitcast_fusion.12
  886.0 11.7 %all-reduce.41 = bf16[512,64]{0,1:T(8,128)(2,1)S(1)} all-reduce(f32[512,64]{0,1:T(8,128)S(1)} %convolution_bitcast_fusion.12), channel_id=1, replica_groups=mesh['adapter'=8,'feature'=4] {'feature'}, use_global_device_ids=true, to_apply=%region_21.24 | all-reduce | flops 32768 | bytes 196608 | tf_op jit(solution)/shard_map/psum | solution.py:80
  897.7 27.0 %all-gather.2.cloned.1.call-done = bf16[128,4096]{1,0:T(8,128)(2,1)} async-done(((bf16[16,4096]{1,0:T(8,128)(2,1)}), bf16[128,4096]{1,0:T(8,128)(2,1)}) %all-gather.2.cloned.1.call-update) | async-done | bytes 1048592 | tf_op jit(solution)/shard_map/all_gather | solution.py:72
  926.5 2.0 convolution_convert_fusion.1
  (102 shorter events, 34.2 us)
Async XLA Ops:
  6.5 877.8 %copy-start = (bf16[512,2048]{1,0:T(8,128)(2,1)S(1)}, bf16[512,2048]{1,0:T(8,128)(2,1)}, u32[]{:S(2)}) copy-start(bf16[512,2048]{1,0:T(8,128)(2,1)} %param.15) | copy-start | bytes 6291460
  6.5 2.6 copy-start.1
  6.5 41.9 %copy-start.10 = (f32[16]{0:T(128)S(1)}, f32[16]{0:T(128)}, u32[]{:S(2)}) copy-start(f32[16]{0:T(128)} %param.12) | copy-start | bytes 196
  6.5 40.0 %all-reduce.40.cloned.1.call-start = ((), (), s32[]{:S(2)}) async-start(), calls=%async_computation.13 | async-start | bytes 524288 | tf_op jit(solution)/shard_map/psum | solution.py:42
  11.3 113.0 %all-reduce.16.cloned.1.call-start = ((), (), s32[]{:S(2)}) async-start(), calls=%async_computation | async-start | bytes 1048576 | tf_op jit(solution)/shard_map/psum | solution.py:36
  51.5 131.2 %copy-start.4 = (f32[16,16,64]{2,1,0:T(8,128)S(1)}, f32[16,16,64]{2,1,0:T(8,128)}, u32[]{:S(2)}) copy-start(f32[16,16,64]{2,1,0:T(8,128)} %get-tuple-element.6) | copy-start | bytes 196612
  51.5 131.2 %all-reduce.18.cloned.1.call-start = ((), (), s32[]{:S(2)}) async-start(), calls=%async_computation.1 | async-start | bytes 262144 | tf_op jit(solution)/shard_map/psum | solution.py:46
  151.4 110.0 %all-reduce.20.cloned.1.call-start = ((), (), s32[]{:S(2)}) async-start(), calls=%async_computation.2 | async-start | bytes 1048576 | tf_op jit(solution)/shard_map/psum | solution.py:36
  188.5 132.6 %copy-start.5 = (f32[16,16,64]{2,1,0:T(8,128)S(1)}, f32[16,16,64]{2,1,0:T(8,128)}, u32[]{:S(2)}) copy-start(f32[16,16,64]{2,1,0:T(8,128)} %all-reduce.18.cloned.1.call-done) | copy-start | bytes 196612
  188.5 132.6 %all-reduce.22.cloned.1.call-start = ((), (), s32[]{:S(2)}) async-start(), calls=%async_computation.3 | async-start | bytes 262144 | tf_op jit(solution)/shard_map/psum | solution.py:42
  289.8 109.1 %all-reduce.24.cloned.1.call-start = ((), (), s32[]{:S(2)}) async-start(), calls=%async_computation.4 | async-start | bytes 1048576 | tf_op jit(solution)/shard_map/psum | solution.py:36
  325.9 131.4 %copy-start.6 = (f32[16,16,64]{2,1,0:T(8,128)S(1)}, f32[16,16,64]{2,1,0:T(8,128)}, u32[]{:S(2)}) copy-start(f32[16,16,64]{2,1,0:T(8,128)} %all-reduce.22.cloned.1.call-done) | copy-start | bytes 196612
  325.9 131.3 %all-reduce.26.cloned.1.call-start = ((), (), s32[]{:S(2)}) async-start(), calls=%async_computation.5 | async-start | bytes 262144 | tf_op jit(solution)/shard_map/psum | solution.py:46
  426.0 110.0 %all-reduce.28.cloned.1.call-start = ((), (), s32[]{:S(2)}) async-start(), calls=%async_computation.6 | async-start | bytes 1048576 | tf_op jit(solution)/shard_map/psum | solution.py:36
  463.1 132.6 %copy-start.7 = (f32[16,16,64]{2,1,0:T(8,128)S(1)}, f32[16,16,64]{2,1,0:T(8,128)}, u32[]{:S(2)}) copy-start(f32[16,16,64]{2,1,0:T(8,128)} %all-reduce.26.cloned.1.call-done) | copy-start | bytes 196612
  463.1 132.6 %all-reduce.30.cloned.1.call-start = ((), (), s32[]{:S(2)}) async-start(), calls=%async_computation.7 | async-start | bytes 262144 | tf_op jit(solution)/shard_map/psum | solution.py:42
  564.4 109.1 %all-reduce.32.cloned.1.call-start = ((), (), s32[]{:S(2)}) async-start(), calls=%async_computation.8 | async-start | bytes 1048576 | tf_op jit(solution)/shard_map/psum | solution.py:36
  600.5 133.5 %copy-start.8 = (f32[16,16,64]{2,1,0:T(8,128)S(1)}, f32[16,16,64]{2,1,0:T(8,128)}, u32[]{:S(2)}) copy-start(f32[16,16,64]{2,1,0:T(8,128)} %all-reduce.30.cloned.1.call-done) | copy-start | bytes 196612
  600.5 133.5 %all-reduce.34.cloned.1.call-start = ((), (), s32[]{:S(2)}) async-start(), calls=%async_computation.9 | async-start | bytes 262144 | tf_op jit(solution)/shard_map/psum | solution.py:46
  701.1 36.4 %copy-start.2 = (bf16[16,16,2048]{2,1,0:T(8,128)(2,1)S(1)}, bf16[16,16,2048]{2,1,0:T(8,128)(2,1)}, u32[]{:S(2)}) copy-start(bf16[16,16,2048]{2,1,0:T(8,128)(2,1)} %param.10) | copy-start | bytes 3145732
  702.8 108.6 %all-reduce.36.cloned.1.call-start = ((), (), s32[]{:S(2)}) async-start(), calls=%async_computation.10 | async-start | bytes 1048576 | tf_op jit(solution)/shard_map/psum | solution.py:36
  738.6 142.8 %copy-start.9 = (f32[16,16,64]{2,1,0:T(8,128)S(1)}, f32[16,16,64]{2,1,0:T(8,128)}, u32[]{:S(2)}) copy-start(f32[16,16,64]{2,1,0:T(8,128)} %all-reduce.34.cloned.1.call-done) | copy-start | bytes 196612
  738.6 142.8 %all-reduce.38.cloned.1.call-start = ((), (), s32[]{:S(2)}) async-start(), calls=%async_computation.11 | async-start | bytes 262144 | tf_op jit(solution)/shard_map/psum | solution.py:42
  846.6 0.7 copy-start.3
  848.4 76.3 %copy-start.11 = (s32[4]{0:T(128)S(1)}, s32[4]{0:T(128)}, u32[]{:S(2)}) copy-start(s32[4]{0:T(128)} %param.16) | copy-start | bytes 52
  850.0 74.7 %all-gather.2.cloned.1.call-start = ((), (), s32[]{:S(2)}) async-start(), calls=%async_computation.12 | async-start | bytes 1179648 | tf_op jit(solution)/shard_map/all_gather | solution.py:72
Sparse Core Ops, SparseCore 0:
  11.4 35.0 all-reduce.39
  51.6 72.6 all-reduce.15
  151.5 31.1 all-reduce.17
  188.6 72.7 all-reduce.19
  289.9 31.1 all-reduce.21
  326.1 72.7 all-reduce.23
  426.1 31.1 all-reduce.25
  463.2 72.7 all-reduce.27
  564.5 31.1 all-reduce.29
  600.6 72.7 all-reduce.31
  702.9 31.1 all-reduce.33
  738.7 72.6 all-reduce.35
  850.2 31.2 all-reduce.37
  884.4 40.2 all-gather.1
where the time goes:
time: 937 us; the launch traced here: 935 us
  waiting for transfers between devices  686 us (73%)
  other arithmetic  79.4 us (8%)
  blocking collectives  74.4 us (8%)
  matrix products  70.3 us (8%)
  between operations  13.7 us (1%)
  local copies, waits for them, and re-layouts  9.93 us (1%)
    psum x6, waiting for transfers between devices, renew(): full_term = lax.psum(local_term, 'adapter')  437 us
    psum x4, waiting for transfers between devices, down_sum(): lax.psum(project(adapter_down, basis_v.astype(jnp.bfloat16)), 'feature')  129 us
    psum x3, waiting for transfers between devices, up_sum(): lax.psum(project(adapter_up, basis_u.astype(jnp.bfloat16)), 'feature')  93.7 us
    psum x6, blocking collectives, renew(): lax.psum(jnp.dot(full_term.T, full_term, precision=highest), 'feature')  62.7 us
    another operation x18, other arithmetic, solve_with(): factor = jnp.linalg.cholesky(gram_sum)  41.3 us
    another operation x12, other arithmetic, solve_with(): lax.linalg.triangular_solve(factor, matrix, left_side=False, lower=True,...  36.7 us
    all_gather x1, waiting for transfers between devices, on_device(): every_core = lax.all_gather(flat_cores, 'adapter', axis=0, tiled=True)  27 us
  transfers between devices with their start and end apart: 14, of which 14 were waited for; matrix products, arithmetic and copies ran while one was open for 0% of the time, Pallas kernels for 0%

commit v1 on v0

--- a/solution.py
+++ b/solution.py
@@ -5,6 +5,11 @@
 
 SWEEPS = 3
 highest = lax.Precision.HIGHEST
+
+
+def add_all(x, axis):
+    parts = lax.all_gather(x, axis)
+    return jnp.sum(parts, axis=0)
 
 
 def project(adapter_stack, basis_low):
@@ -39,7 +44,7 @@
 
 
 def down_sum(adapter_down, basis_v):
-    return lax.psum(project(adapter_down, basis_v.astype(jnp.bfloat16)), "feature")
+    return add_all(project(adapter_down, basis_v.astype(jnp.bfloat16)), "feature")
 
 
 def up_sum(adapter_up, basis_u):

time: 937 us -> 855 us (0.912)
  waiting for transfers between devices: 686 us -> 576 us
  blocking collectives: 74.4 us -> 108 us
    psum x4 -> x0, waiting for transfers between devices: 129 us -> none  [down_sum(): lax.psum(project(adapter_down, basis_v.astype(jnp.bfloat16)), 'feature')]
    all_gather x0 -> x4, blocking collectives: none -> 32.7 us  [add_all(): parts = lax.all_gather(x, axis)]
    psum x3 -> x4, waiting for transfers between devices: 93.7 us -> 117 us  [up_sum(): lax.psum(project(adapter_up, basis_u.astype(jnp.bfloat16)), 'feature')]
  transfers between devices with their start and end apart: 14 -> 11, of which waited for: 14 -> 11; matrix products, arithmetic and copies ran while one was open for 0% -> 0% of each run, Pallas kernels for 0% -> 0%
where the time goes in v1:
time: 855 us; the launch traced here: 853 us
  waiting for transfers between devices  576 us (67%)
  blocking collectives  108 us (13%)
  other arithmetic  82.7 us (10%)
  matrix products  63.6 us (7%)
  between operations  13.7 us (2%)
    psum x6, waiting for transfers between devices, renew(): full_term = lax.psum(local_term, 'adapter')  434 us
    psum x4, waiting for transfers between devices, up_sum(): lax.psum(project(adapter_up, basis_u.astype(jnp.bfloat16)), 'feature')  117 us
    psum x6, blocking collectives, renew(): lax.psum(jnp.dot(full_term.T, full_term, precision=highest), 'feature')  63.1 us
    another operation x18, other arithmetic, solve_with(): factor = jnp.linalg.cholesky(gram_sum)  41.3 us
    another operation x12, other arithmetic, solve_with(): lax.linalg.triangular_solve(factor, matrix, left_side=False, lower=True,...  36.7 us
    all_gather x4, blocking collectives, add_all(): parts = lax.all_gather(x, axis)  32.7 us
    all_gather x1, waiting for transfers between devices, on_device(): every_core = lax.all_gather(flat_cores, 'adapter', axis=0, tiled=True)  25.5 us
  transfers between devices with their start and end apart: 11, of which 11 were waited for; matrix products, arithmetic and copies ran while one was open for 0% of the time, Pallas kernels for 0%

profile of v1, /device:TPU:0, one launch (start us, length us, event | category | flops | bytes accessed | tf_op | source)
XLA Modules:
  0.0 853.2 jit_solution(13234210544477942177)
XLA Ops:
  6.5 2.6 fusion.13
  9.2 1.9 fusion.15
  11.1 9.1 %all-gather = f32[64,16,64]{2,1,0:T(8,128)} all-gather(f32[16,16,64]{2,1,0:T(8,128)S(1)} %fusion.15), channel_id=2, replica_groups=mesh['adapter'=8,'feature'=4] {'feature'}, dimensions={0}, use_global_device_ids=true | all-gather | bytes 327680 | tf_op jit(solution)/shard_map/all_gather | solution.py:11
  21.3 22.9 %all-reduce.12.cloned.1.call-done = f32[16,16,64]{2,1,0:T(8,128)} async-done(((f32[16,16,64]{2,1,0:T(8,128)}), f32[16,16,64]{2,1,0:T(8,128)}) %all-reduce.12.cloned.1.call-update) | async-done | bytes 65552 | tf_op jit(solution)/shard_map/psum | solution.py:51
  44.2 1.9 fusion.52
  48.2 72.9 %all-reduce.14.cloned.1.call-done = f32[2048,64]{0,1:T(8,128)} async-done(((f32[2048,64]{0,1:T(8,128)}), f32[2048,64]{0,1:T(8,128)}) %all-reduce.14.cloned.1.call-update) | async-done | bytes 524304 | tf_op jit(solution)/shard_map/psum | solution.py:41
  121.1 1.8 fusion.53
  122.9 10.3 %psum.121 = f32[64,64]{0,1:T(8,128)S(1)} all-reduce(f32[64,64]{0,1:T(8,128)S(1)} %fusion.53), channel_id=1, replica_groups=mesh['adapter'=8,'feature'=4] {'feature'}, use_global_device_ids=true, to_apply=%region_3.0 | all-reduce | flops 4096 | bytes 32768 | tf_op jit(solution)/shard_map/psum | solution.py:42
  133.3 5.8 cholesky.104
  140.5 4.9 custom-call.10
  145.3 1.7 fusion
  148.3 31.2 %all-reduce.16.cloned.1.call-done = f32[16,16,64]{2,1,0:T(8,128)} async-done(((f32[16,16,64]{2,1,0:T(8,128)}), f32[16,16,64]{2,1,0:T(8,128)}) %all-reduce.16.cloned.1.call-update) | async-done | bytes 65552 | tf_op jit(solution)/shard_map/psum | solution.py:51
  179.5 1.9 fusion.54
  181.5 1.5 fusion.7
  182.9 2.3 convolution_bitcast_fusion.10
  185.3 72.7 %all-reduce.18.cloned.1.call-done = f32[2048,64]{0,1:T(8,128)} async-done(((f32[2048,64]{0,1:T(8,128)}), f32[2048,64]{0,1:T(8,128)}) %all-reduce.18.cloned.1.call-update) | async-done | bytes 524304 | tf_op jit(solution)/shard_map/psum | solution.py:41
  258.1 1.8 fusion.55
  259.9 10.4 %psum.124 = f32[64,64]{0,1:T(8,128)S(1)} all-reduce(f32[64,64]{0,1:T(8,128)S(1)} %fusion.55), channel_id=1, replica_groups=mesh['adapter'=8,'feature'=4] {'feature'}, use_global_device_ids=true, to_apply=%region_8.11 | all-reduce | flops 4096 | bytes 32768 | tf_op jit(solution)/shard_map/psum | solution.py:42
  270.4 5.8 cholesky.115
  277.6 4.9 custom-call.11
  282.5 1.7 fusion.1
  284.1 1.7 convolution_bitcast_fusion.17
  285.9 7.9 all_gather.16
  298.1 71.4 %all-reduce.20.cloned.1.call-done = f32[2048,64]{0,1:T(8,128)} async-done(((f32[2048,64]{0,1:T(8,128)}), f32[2048,64]{0,1:T(8,128)}) %all-reduce.20.cloned.1.call-update) | async-done | bytes 524304 | tf_op jit(solution)/shard_map/psum | solution.py:41
  369.5 1.8 fusion.57
  371.3 10.3 %psum.126 = f32[64,64]{0,1:T(8,128)S(1)} all-reduce(f32[64,64]{0,1:T(8,128)S(1)} %fusion.57), channel_id=1, replica_groups=mesh['adapter'=8,'feature'=4] {'feature'}, use_global_device_ids=true, to_apply=%region_11.14 | all-reduce | flops 4096 | bytes 32768 | tf_op jit(solution)/shard_map/psum | solution.py:42
  381.7 5.8 cholesky.126
  388.8 4.9 custom-call.12
  393.7 1.7 fusion.2
  396.7 31.2 %all-reduce.22.cloned.1.call-done = f32[16,16,64]{2,1,0:T(8,128)} async-done(((f32[16,16,64]{2,1,0:T(8,128)}), f32[16,16,64]{2,1,0:T(8,128)}) %all-reduce.22.cloned.1.call-update) | async-done | bytes 65552 | tf_op jit(solution)/shard_map/psum | solution.py:51
  427.9 1.9 fusion.58
  429.9 1.5 fusion.9
  431.3 2.3 convolution_bitcast_fusion.8
  433.7 72.9 %all-reduce.24.cloned.1.call-done = f32[2048,64]{0,1:T(8,128)} async-done(((f32[2048,64]{0,1:T(8,128)}), f32[2048,64]{0,1:T(8,128)}) %all-reduce.24.cloned.1.call-update) | async-done | bytes 524304 | tf_op jit(solution)/shard_map/psum | solution.py:41
  506.6 1.8 fusion.59
  508.4 10.4 %psum.129 = f32[64,64]{0,1:T(8,128)S(1)} all-reduce(f32[64,64]{0,1:T(8,128)S(1)} %fusion.59), channel_id=1, replica_groups=mesh['adapter'=8,'feature'=4] {'feature'}, use_global_device_ids=true, to_apply=%region_14.17 | all-reduce | flops 4096 | bytes 32768 | tf_op jit(solution)/shard_map/psum | solution.py:42
  518.9 5.8 cholesky.137
  526.1 4.9 custom-call.13
  531.0 1.7 fusion.3
  532.7 1.7 convolution_bitcast_fusion.15
  534.5 8.0 all_gather.17
  546.7 71.4 %all-reduce.26.cloned.1.call-done = f32[2048,64]{0,1:T(8,128)} async-done(((f32[2048,64]{0,1:T(8,128)}), f32[2048,64]{0,1:T(8,128)}) %all-reduce.26.cloned.1.call-update) | async-done | bytes 524304 | tf_op jit(solution)/shard_map/psum | solution.py:41
  618.1 1.8 fusion.61
  619.9 10.3 %psum.131 = f32[64,64]{0,1:T(8,128)S(1)} all-reduce(f32[64,64]{0,1:T(8,128)S(1)} %fusion.61), channel_id=1, replica_groups=mesh['adapter'=8,'feature'=4] {'feature'}, use_global_device_ids=true, to_apply=%region_17.20 | all-reduce | flops 4096 | bytes 32768 | tf_op jit(solution)/shard_map/psum | solution.py:42
  630.2 5.8 cholesky.148
  637.4 5.5 custom-call.14
  643.0 1.7 fusion.4
  645.7 1.7 copy.56
  647.5 31.2 %all-reduce.28.cloned.1.call-done = f32[16,16,64]{2,1,0:T(8,128)} async-done(((f32[16,16,64]{2,1,0:T(8,128)}), f32[16,16,64]{2,1,0:T(8,128)}) %all-reduce.28.cloned.1.call-update) | async-done | bytes 65552 | tf_op jit(solution)/shard_map/psum | solution.py:51
  678.7 1.9 fusion.62
  680.6 1.5 fusion.11
  683.3 72.7 %all-reduce.30.cloned.1.call-done = f32[2048,64]{0,1:T(8,128)} async-done(((f32[2048,64]{0,1:T(8,128)}), f32[2048,64]{0,1:T(8,128)}) %all-reduce.30.cloned.1.call-update) | async-done | bytes 524304 | tf_op jit(solution)/shard_map/psum | solution.py:41
  756.0 2.4 fusion.63
  758.4 11.5 %psum.134 = f32[64,64]{0,1:T(8,128)} all-reduce(f32[64,64]{0,1:T(8,128)} %fusion.63), channel_id=1, replica_groups=mesh['adapter'=8,'feature'=4] {'feature'}, use_global_device_ids=true, to_apply=%region_20.23 | all-reduce | flops 4096 | bytes 32768 | tf_op jit(solution)/shard_map/psum | solution.py:42
  769.9 1.4 copy.58
  772.8 7.2 cholesky.159
  781.4 2.0 fusion.28
  783.5 6.3 custom-call.15
  789.7 1.7 fusion.5
  794.2 7.7 all_gather.18
  804.7 12.6 %all-reduce.31 = bf16[512,64]{0,1:T(8,128)(2,1)S(1)} all-reduce(f32[512,64]{0,1:T(8,128)S(1)} %convolution_bitcast_fusion.12), channel_id=1, replica_groups=mesh['adapter'=8,'feature'=4] {'feature'}, use_global_device_ids=true, to_apply=%region_21.24 | all-reduce | flops 32768 | bytes 196608 | tf_op jit(solution)/shard_map/psum | solution.py:85
  817.3 25.5 %all-gather.3.cloned.1.call-done = bf16[128,4096]{1,0:T(8,128)(2,1)} async-done(((bf16[16,4096]{1,0:T(8,128)(2,1)}), bf16[128,4096]{1,0:T(8,128)(2,1)}) %all-gather.3.cloned.1.call-update) | async-done | bytes 1048592 | tf_op jit(solution)/shard_map/all_gather | solution.py:77
  842.9 1.5 convolution_convert_fusion
  844.7 2.0 convolution_convert_fusion.1
  (97 shorter events, 32.5 us)
Async XLA Ops:
  6.5 797.4 %copy-start = (bf16[512,2048]{1,0:T(8,128)(2,1)S(1)}, bf16[512,2048]{1,0:T(8,128)(2,1)}, u32[]{:S(2)}) copy-start(bf16[512,2048]{1,0:T(8,128)(2,1)} %param.15) | copy-start | bytes 6291460
  6.5 37.7 %all-reduce.12.cloned.1.call-start = ((), (), s32[]{:S(2)}) async-start(), calls=%async_computation | async-start | bytes 262144 | tf_op jit(solution)/shard_map/psum | solution.py:51
  9.1 37.0 %copy-start.8 = (f32[16]{0:T(128)S(1)}, f32[16]{0:T(128)}, u32[]{:S(2)}) copy-start(f32[16]{0:T(128)} %param.12) | copy-start | bytes 196
  9.2 37.9 %copy-start.1 = (bf16[16,16,2048]{2,1,0:T(8,128)(2,1)S(1)}, bf16[16,16,2048]{2,1,0:T(8,128)(2,1)}, u32[]{:S(2)}) copy-start(bf16[16,16,2048]{2,1,0:T(8,128)(2,1)} %param.11) | copy-start | bytes 3145732
  9.2 112.0 %all-reduce.14.cloned.1.call-start = ((), (), s32[]{:S(2)}) async-start(), calls=%async_computation.1 | async-start | bytes 1048576 | tf_op jit(solution)/shard_map/psum | solution.py:41
  48.2 131.4 %all-reduce.16.cloned.1.call-start = ((), (), s32[]{:S(2)}) async-start(), calls=%async_computation.2 | async-start | bytes 262144 | tf_op jit(solution)/shard_map/psum | solution.py:51
  148.3 109.8 %all-reduce.18.cloned.1.call-start = ((), (), s32[]{:S(2)}) async-start(), calls=%async_computation.3 | async-start | bytes 1048576 | tf_op jit(solution)/shard_map/psum | solution.py:41
  185.3 184.2 %all-reduce.20.cloned.1.call-start = ((), (), s32[]{:S(2)}) async-start(), calls=%async_computation.4 | async-start | bytes 1048576 | tf_op jit(solution)/shard_map/psum | solution.py:41
  259.9 35.1 %copy-start.5 = (f32[16,16,64]{2,1,0:T(8,128)S(1)}, f32[16,16,64]{2,1,0:T(8,128)}, u32[]{:S(2)}) copy-start(f32[16,16,64]{2,1,0:T(8,128)} %all-reduce.16.cloned.1.call-done) | copy-start | bytes 196612
  298.0 129.9 %all-reduce.22.cloned.1.call-start = ((), (), s32[]{:S(2)}) async-start(), calls=%async_computation.5 | async-start | bytes 262144 | tf_op jit(solution)/shard_map/psum | solution.py:51
  396.6 110.0 %all-reduce.24.cloned.1.call-start = ((), (), s32[]{:S(2)}) async-start(), calls=%async_computation.6 | async-start | bytes 1048576 | tf_op jit(solution)/shard_map/psum | solution.py:41
  433.7 184.4 %all-reduce.26.cloned.1.call-start = ((), (), s32[]{:S(2)}) async-start(), calls=%async_computation.7 | async-start | bytes 1048576 | tf_op jit(solution)/shard_map/psum | solution.py:41
  508.4 35.1 %copy-start.6 = (f32[16,16,64]{2,1,0:T(8,128)S(1)}, f32[16,16,64]{2,1,0:T(8,128)}, u32[]{:S(2)}) copy-start(f32[16,16,64]{2,1,0:T(8,128)} %all-reduce.22.cloned.1.call-done) | copy-start | bytes 196612
  546.6 132.1 %all-reduce.28.cloned.1.call-start = ((), (), s32[]{:S(2)}) async-start(), calls=%async_computation.8 | async-start | bytes 262144 | tf_op jit(solution)/shard_map/psum | solution.py:51
  645.7 36.4 %copy-start.2 = (bf16[16,16,2048]{2,1,0:T(8,128)(2,1)S(1)}, bf16[16,16,2048]{2,1,0:T(8,128)(2,1)}, u32[]{:S(2)}) copy-start(bf16[16,16,2048]{2,1,0:T(8,128)(2,1)} %param.10) | copy-start | bytes 3145732
  647.4 108.6 %all-reduce.30.cloned.1.call-start = ((), (), s32[]{:S(2)}) async-start(), calls=%async_computation.9 | async-start | bytes 1048576 | tf_op jit(solution)/shard_map/psum | solution.py:41
  683.2 159.6 %all-gather.3.cloned.1.call-start = ((), (), s32[]{:S(2)}) async-start(), calls=%async_computation.10 | async-start | bytes 1179648 | tf_op jit(solution)/shard_map/all_gather | solution.py:77
  758.4 43.5 %copy-start.7 = (f32[16,16,64]{2,1,0:T(8,128)S(1)}, f32[16,16,64]{2,1,0:T(8,128)}, u32[]{:S(2)}) copy-start(f32[16,16,64]{2,1,0:T(8,128)} %all-reduce.28.cloned.1.call-done) | copy-start | bytes 196612
  791.4 0.7 copy-start.3
  793.2 10.7 %copy-start.4 = (bf16[2048,64]{0,1:T(8,128)(2,1)S(1)}, bf16[2048,64]{0,1:T(8,128)(2,1)}, u32[]{:S(2)}) copy-start(bf16[2048,64]{0,1:T(8,128)(2,1)} %copy-done.3) | copy-start | bytes 786436
  801.9 41.0 %copy-start.9 = (s32[4]{0:T(128)S(1)}, s32[4]{0:T(128)}, u32[]{:S(2)}) copy-start(s32[4]{0:T(128)} %param.16) | copy-start | bytes 52
Sparse Core Ops, SparseCore 0:
  9.6 34.4 all-reduce.11
  48.3 72.7 all-reduce.13
  148.4 31.1 all-reduce.15
  185.4 72.6 all-reduce.17
  298.2 71.3 all-reduce.19
  396.8 31.1 all-reduce.21
  433.8 72.7 all-reduce.23
  546.7 71.3 all-reduce.25
  647.5 31.1 all-reduce.27
  683.4 72.6 all-reduce.29
  804.0 38.8 all-gather.2
